TPU v7x, 256 devices: a whole 4x4x8 slice. The times are simulated.
256 devices in a mesh: wire: 64 (over z, y, core), col: 4 (over x).
Axes of the slice: x: 4, y: 4, z: 8, core: 2. Of those that a mesh axis runs over, the one named last changes fastest.
Arguments:
- search: float32 [196608, 384], P('wire', 'col')
- block_values: float32 [196608, 256], P('wire'), may hold values from -0.375 to 0.375
- block_cols: int32 [3072, 4], P('wire'), may hold values from 0 to 3071, as said below
- ritz: float32 [384, 128], replicated, may hold values from -0.3125 to 0.3125
Outputs:
- new_modes: float32 [196608, 128], P('wire', 'col')
- residual: float32 [196608, 128], P('wire', 'col')
- theta: float32 [128], P('col')
- gram_stiff: float32 [384, 384], P(None, 'col')
- gram_mass: float32 [384, 384], P(None, 'col')
Inputs may be any that keep to these rules, and one draw needn't show every extreme that they name: Block rows are in groups of 48, b in group g = b // 48. block_cols[b, 0] = b. Column 1 names a block row of group g. For even b, column 2 names a block row of group g + 1 and column 3 one of group g + 2; for odd b, groups g - 1 and g - 2; groups counted around the loop of all groups.
All inputs are finite; a program needn't handle non-finite values.
Results may differ from a plain program's by a relative error of at most 0.0003.
Values sent between devices are 32-bit elements; how exact they have to be, the bound alone decides.
No kernel may reach another device: no remote copies, remote signals or barrier semaphores. Data moves between devices by JAX's collectives and lax.ppermute only.
A program may use at most 64 MiB of HBM per device.

v0:
```python
import jax
import jax.numpy as jnp
from jax import lax
from jax.sharding import PartitionSpec as P


def shifted(array, axis, by):
    length = lax.axis_size(axis)
    return lax.ppermute(array, axis, [(i, (i + by) % length) for i in range(length)])


def neighbour_group(search, distance):
    return shifted(search, "wire", distance)


def shards(search, block_values, block_cols, ritz):
    high = lax.Precision.HIGHEST
    rows, width = search.shape
    blk = block_cols.shape[0]
    block = rows // blk
    slots = block_cols.shape[1]
    col_here = lax.axis_index("col")
    wire_here = lax.axis_index("wire")
    wire_count = lax.axis_size("wire")
    extended = jnp.concatenate(
        [
            neighbour_group(search, 2),
            neighbour_group(search, 1),
            search,
            neighbour_group(search, -1),
            neighbour_group(search, -2),
        ],
        axis=0,
    )
    ext_blocks = extended.reshape(5 * blk, block, width)
    owner = block_cols // blk
    offset = (owner - wire_here + 2 + wire_count) % wire_count
    local_index = offset * blk + block_cols % blk
    picked = ext_blocks[local_index].reshape(blk, slots * block, width)
    values = block_values.reshape(blk, block, slots * block)
    product = jnp.einsum("bik,bkc->bic", values, picked, precision=high).reshape(rows, width)
    image = 4.0 * search + product
    paired = jnp.concatenate([image, search], axis=1)
    partial_gram = jnp.einsum(
        "rk,rc->kc", lax.all_gather(search, "col", axis=1, tiled=True), paired, precision=high
    )
    mine = lax.dynamic_slice_in_dim(ritz, col_here * width, width, 0)
    modes_part = jnp.dot(search, mine, precision=high, preferred_element_type=jnp.float32)
    image_part = jnp.dot(image, mine, precision=high, preferred_element_type=jnp.float32)
    new_modes, new_image = (
        lax.psum_scatter(modes_part, "col", scatter_dimension=1, tiled=True),
        lax.psum_scatter(image_part, "col", scatter_dimension=1, tiled=True),
    )
    total_rows = jnp.float32(rows * wire_count)
    gram_total = lax.psum(partial_gram, "wire") / total_rows
    gram_stiff = gram_total[:, :width]
    gram_mass = gram_total[:, width:]
    mine_rows = lax.dynamic_slice_in_dim(ritz, col_here * width, width, 0)
    left_stiff = jnp.einsum("ab,aj->jb", gram_stiff, ritz, precision=high)
    left_mass = jnp.einsum("ab,aj->jb", gram_mass, ritz, precision=high)
    numer_terms = jnp.sum(left_stiff * mine_rows.T, axis=1)
    denom_terms = jnp.sum(left_mass * mine_rows.T, axis=1)
    sums = lax.psum_scatter(
        jnp.stack([numer_terms, denom_terms]), "col", scatter_dimension=1, tiled=True
    )
    theta = sums[0] / sums[1]
    residual = new_image - new_modes * theta[None, :]
    return (new_modes, residual, theta, gram_stiff, gram_mass)


def solution(mesh):
    placed = (P("wire", "col"), P("wire", None), P("wire", None), P())
    return jax.shard_map(
        shards,
        mesh=mesh,
        in_specs=placed,
        out_specs=(P("wire", "col"), P("wire", "col"), P("col"), P(None, "col"), P(None, "col")),
        check_vma=False,
    )
```

profile of v0, /device:TPU:1, one launch (start us, length us, event | category | flops | bytes accessed | tf_op | source)
XLA Modules:
  0.0 370.5 jit_solution(8601047787876571192)
XLA Ops:
  7.2 0.7 all-gather.2.cloned.1.call-update
  8.0 2.2 collective-permute-start
  10.2 2.1 collective-permute-start.1
  12.3 5.5 %collective-permute-start.3 = (f32[3072,96]{0,1:T(8,128)}, f32[3072,96]{0,1:T(8,128)}, u32[]{:S(2)}, u32[]{:S(2)}) collective-permute-start(f32[3072,96]{0,1:T(8,128)} %param.4), channel_id=1, source_target_pairs={{0,248},{4,252},{8,0},{12,4},{16,8},{20,12},{24,16},{28,20},{32,24... | collective-permute-start | bytes 3538952 | tf_op jit(solution)/shard_map/ppermute | solution.py:9
  17.7 0.7 compare_select_fusion
  18.5 0.1 reshape.29
  18.7 24.2 %collective-permute-done = f32[3072,96]{0,1:T(8,128)} collective-permute-done((f32[3072,96]{0,1:T(8,128)}, f32[3072,96]{0,1:T(8,128)}, u32[]{:S(2)}, u32[]{:S(2)}) %collective-permute-start) | collective-permute-done | bytes 1179680 | tf_op jit(solution)/shard_map/ppermute | solution.py:9
  42.9 2.4 constant_dynamic-update-slice_fusion.4
  45.2 3.7 collective-permute-done.1
  48.9 2.4 constant_dynamic-update-slice_fusion.3
  51.3 1.1 constant_dynamic-update-slice_fusion.2
  52.4 2.4 constant_dynamic-update-slice_fusion.1
  54.8 2.4 constant_dynamic-update-slice_fusion
  57.2 8.2 %copy.14 = f32[15360,96]{1,0:T(8,128)} copy(f32[15360,96]{0,1:T(8,128)} %constant_dynamic-update-slice_fusion) | data formatting | bytes 11796480 | tf_op jit(solution)/shard_map/concatenate | solution.py:25
  65.3 6.9 %gather_fusion = f32[192,64,96]{2,1,0:T(8,128)} fusion(f32[240,64,96]{2,1,0:T(8,128)} %bitcast.26, s32[1024]{0:T(1024)S(1)} %pad_clamp_fusion), kind=kCustom, calls=%fused_computation | custom fusion | bytes 9437952 | tf_op jit(solution)/shard_map/gather | solution.py:39
  72.2 7.2 %fusion.21 = f32[48,96,64]{1,2,0:T(8,128)} fusion(f32[48,256,96]{2,1,0:T(8,128)} %bitcast.27, f32[48,64,256]{2,1,0:T(8,128)S(1)} %bitcast.25), kind=kOutput, calls=%fused_computation.41 | convolution fusion | flops 905969664 | bytes 9043968 | tf_op jit(solution)/shard_map/bik,bkc->bic/dot_general | solution.py:41
  79.5 2.9 copy.17
  82.4 2.8 multiply_add_fusion
  85.2 8.7 %fusion.4 = f32[384,192]{0,1:T(8,128)} fusion(f32[3072,384]{0,1:T(8,128)} %all-gather.2.cloned.1.call-done, f32[3072,96]{0,1:T(8,128)} %param.4, f32[3072,96]{0,1:T(8,128)} %multiply_add_fusion), kind=kOutput, calls=%fused_computation.7 | convolution fusion | flops 2718498816 | bytes 7372800 | tf_op jit(solution)/shard_map/rk,rc->kc/dot_general | solution.py:44
  93.9 182.5 %all-reduce.2.cloned.1.call-done = f32[384,192]{0,1:T(8,128)} async-done(((f32[384,192]{0,1:T(8,128)}), f32[384,192]{0,1:T(8,128)}) %all-reduce.2.cloned.1.call-update) | async-done | bytes 294928 | tf_op jit(solution)/shard_map/psum | solution.py:55
  276.4 1.0 broadcast_multiply_fusion
  277.4 0.3 fusion.7
  277.8 0.3 copy-done.4
  278.1 0.3 fusion.8
  278.4 0.7 copy.19
  279.2 3.9 %convolution_bitcast_fusion = f32[3072,128]{0,1:T(8,128)} fusion(f32[3072,96]{0,1:T(8,128)} %param.4, f32[384,128]{1,0:T(8,128)S(1)} %copy-done.2, s32[]{:T(128)S(6)} %select_n.23), kind=kOutput, calls=%fused_computation.1 | convolution fusion | flops 452984832 | bytes 2801668 | tf_op jit(solution)/shard_map/dot_general | solution.py:48
  283.2 3.9 %fusion.9 = f32[3072,128]{0,1:T(8,128)} fusion(f32[3072,96]{0,1:T(8,128)} %multiply_add_fusion, f32[384,128]{1,0:T(8,128)S(1)} %copy-done.2, s32[]{:T(128)S(6)} %select_n.23), kind=kOutput, calls=%fused_computation.14 | convolution fusion | flops 452984832 | bytes 2801668 | tf_op jit(solution)/shard_map/dot_general | solution.py:49
  287.0 12.1 %reduce-scatter.10.cloned.1.call-done = f32[32,2]{1,0:T(8,128)} async-done(((f32[128,2]{1,0:T(8,128)}), f32[32,2]{1,0:T(8,128)}) %reduce-scatter.10.cloned.1.call-update) | async-done | bytes 272
  299.2 0.9 fusion.20
  300.2 31.4 %reduce-scatter.6.cloned.1.call-done = f32[3072,32]{0,1:T(8,128)} async-done(((f32[3072,128]{0,1:T(8,128)}), f32[3072,32]{0,1:T(8,128)}) %reduce-scatter.6.cloned.1.call-update) | async-done | bytes 393232 | tf_op jit(solution)/shard_map/reduce_scatter | solution.py:51
  331.6 30.4 %reduce-scatter.8.cloned.1.call-done = f32[3072,32]{0,1:T(8,128)} async-done(((f32[3072,128]{0,1:T(8,128)}), f32[3072,32]{0,1:T(8,128)}) %reduce-scatter.8.cloned.1.call-update) | async-done | bytes 393232 | tf_op jit(solution)/shard_map/reduce_scatter | solution.py:52
  362.0 2.0 multiply_subtract_fusion
  (31 shorter events, 0.6 us)
Async XLA Ops:
  7.2 65.0 %copy-start = (f32[3072,256]{1,0:T(8,128)S(1)}, f32[3072,256]{1,0:T(8,128)}, u32[]{:S(2)}) copy-start(f32[3072,256]{1,0:T(8,128)} %param.5) | copy-start | bytes 9437188
  7.2 78.0 %all-gather.2.cloned.1.call-start = ((), (), s32[]{:S(2)}) async-start(), calls=%async_computation.5 | async-start | bytes 5898240 | tf_op jit(solution)/shard_map/all_gather | solution.py:45
  7.9 268.5 %all-reduce.2.cloned.1.call-start = ((), (), s32[]{:S(2)}) async-start(), calls=%async_computation.6 | async-start | bytes 589824 | tf_op jit(solution)/shard_map/psum | solution.py:55
  8.0 34.9 %collective-permute-start = (f32[3072,96]{0,1:T(8,128)}, f32[3072,96]{0,1:T(8,128)}, u32[]{:S(2)}, u32[]{:S(2)}) collective-permute-start(f32[3072,96]{0,1:T(8,128)} %param.4), channel_id=1, source_target_pairs={{0,8},{4,12},{8,16},{12,20},{16,24},{20,28},{24,32},{28,36},{32,40... | collective-permute-start | bytes 3538952 | tf_op jit(solution)/shard_map/ppermute | solution.py:9
  10.2 38.7 %collective-permute-start.1 = (f32[3072,96]{0,1:T(8,128)}, f32[3072,96]{0,1:T(8,128)}, u32[]{:S(2)}, u32[]{:S(2)}) collective-permute-start(f32[3072,96]{0,1:T(8,128)} %param.4), channel_id=1, source_target_pairs={{0,4},{4,8},{8,12},{12,16},{16,20},{20,24},{24,28},{28,32},{32,36}... | collective-permute-start | bytes 3538952 | tf_op jit(solution)/shard_map/ppermute | solution.py:9
  12.3 40.1 %collective-permute-start.2 = (f32[3072,96]{0,1:T(8,128)}, f32[3072,96]{0,1:T(8,128)}, u32[]{:S(2)}, u32[]{:S(2)}) collective-permute-start(f32[3072,96]{0,1:T(8,128)} %param.4), channel_id=1, source_target_pairs={{0,252},{4,0},{8,4},{12,8},{16,12},{20,16},{24,20},{28,24},{32,28}... | collective-permute-start | bytes 3538952 | tf_op jit(solution)/shard_map/ppermute | solution.py:9
  12.3 42.5 %collective-permute-start.3 = (f32[3072,96]{0,1:T(8,128)}, f32[3072,96]{0,1:T(8,128)}, u32[]{:S(2)}, u32[]{:S(2)}) collective-permute-start(f32[3072,96]{0,1:T(8,128)} %param.4), channel_id=1, source_target_pairs={{0,248},{4,252},{8,0},{12,4},{16,8},{20,12},{24,16},{28,20},{32,24... | collective-permute-start | bytes 3538952 | tf_op jit(solution)/shard_map/ppermute | solution.py:9
  18.7 32.6 %copy-start.1 = (f32[3072,96]{0,1:T(8,128)S(1)}, f32[3072,96]{0,1:T(8,128)}, u32[]{:S(2)}) copy-start(f32[3072,96]{0,1:T(8,128)} %param.4) | copy-start | bytes 3538948
  85.2 192.3 %copy-start.2 = (f32[384,128]{1,0:T(8,128)S(1)}, f32[384,128]{1,0:T(8,128)}, u32[]{:S(2)}) copy-start(f32[384,128]{1,0:T(8,128)} %param.7) | copy-start | bytes 589828
  93.9 205.3 %reduce-scatter.10.cloned.1.call-start = ((), (), s32[]{:S(2)}) async-start(), calls=%async_computation.7 | async-start | bytes 81920
  277.4 0.7 copy-start.4
  277.4 5.7 %copy-start.3 = (f32[384,96]{0,1:T(8,128)}, f32[384,96]{0,1:T(8,128)S(1)}, u32[]{:S(2)}) copy-start(f32[384,96]{0,1:T(8,128)S(1)} %get-tuple-element.5) | copy-start | bytes 442372
  279.2 52.4 %reduce-scatter.6.cloned.1.call-start = ((), (), s32[]{:S(2)}) async-start(), calls=%async_computation.3 | async-start | bytes 1966080 | tf_op jit(solution)/shard_map/reduce_scatter | solution.py:51
  283.1 78.9 %reduce-scatter.8.cloned.1.call-start = ((), (), s32[]{:S(2)}) async-start(), calls=%async_computation.4 | async-start | bytes 1966080 | tf_op jit(solution)/shard_map/reduce_scatter | solution.py:52
  300.2 63.8 %copy-start.5 = (f32[32]{0:T(128)}, f32[32]{0:T(128)S(1)}, u32[]{:S(2)}) copy-start(f32[32]{0:T(128)S(1)} %divide_bitcast_fusion) | copy-start | bytes 388
Sparse Core Ops, SparseCore 0:
  9.8 58.6 all-gather.1
  94.0 182.3 all-reduce.1
  279.5 19.6 reduce-scatter.9
  302.1 29.3 reduce-scatter.5
  334.0 28.0 reduce-scatter.7
where the time goes:
time: 371 us
  waiting for transfers between devices  285 us (77%)
  local copies, waits for them, and re-layouts  30.9 us (8%)
  matrix products  24.2 us (7%)
  between operations  13.9 us (4%)
  starting transfers between devices  9.98 us (3%)
  other arithmetic  6.48 us (2%)
    psum x1, waiting for transfers between devices, shards(): gram_total = lax.psum(partial_gram, 'wire') / total_rows  182 us
    reduce_scatter x1, waiting for transfers between devices, shards(): lax.psum_scatter(modes_part, 'col', scatter_dimension=1, tiled=True)  31.4 us
    reduce_scatter x1, waiting for transfers between devices, shards(): lax.psum_scatter(image_part, 'col', scatter_dimension=1, tiled=True)  30.4 us
    ppermute x4, waiting for transfers between devices, shifted(): lax.ppermute(array, axis, [(i, (i + by) % length) for i in range(length)])  27.9 us
    unnamed x6, waiting for transfers between devices  12.9 us
    concatenate x2, local copies, waits for them, and re-layouts, shards(): jnp.concatenate([neighbour_group(search, 2), neighbour_group(search, 1),...  10.5 us
    ppermute x4, starting transfers between devices, shifted(): lax.ppermute(array, axis, [(i, (i + by) % length) for i in range(length)])  9.78 us
    unnamed x19, local copies, waits for them, and re-layouts  9.5 us
  transfers between devices with their start and end apart: 9, of which 6 were waited for; matrix products, arithmetic and copies ran while one was open for 13% of the time, Pallas kernels for 0%

commit v1 on v0

--- a/solution.py
+++ b/solution.py
@@ -1,7 +1,7 @@
 import jax
 import jax.numpy as jnp
 from jax import lax
-from jax.sharding import PartitionSpec as P
+from jax.sharding import Mesh, PartitionSpec as P
 
 
 def shifted(array, axis, by):
@@ -9,8 +9,22 @@
     return lax.ppermute(array, axis, [(i, (i + by) % length) for i in range(length)])
 
 
+RING = ("y", "core")
+WIRE = ("z", "y", "core")
+
+
+def sum_over_wire(x):
+    shape = x.shape
+    flat = x.reshape(8, -1, 128)
+    part = jnp.sum(lax.all_to_all(flat, RING, 0, 0, tiled=True), axis=0)
+    spread = jnp.broadcast_to(part[None], (8,) + part.shape)
+    part = jnp.sum(lax.all_to_all(spread, "z", 0, 0, tiled=True), axis=0)
+    spread = jnp.broadcast_to(part[None], (8,) + part.shape)
+    return lax.all_to_all(spread, RING, 0, 0, tiled=True).reshape(shape)
+
+
 def neighbour_group(search, distance):
-    return shifted(search, "wire", distance)
+    return shifted(search, WIRE, distance)
 
 
 def shards(search, block_values, block_cols, ritz):
@@ -20,8 +34,8 @@
     block = rows // blk
     slots = block_cols.shape[1]
     col_here = lax.axis_index("col")
-    wire_here = lax.axis_index("wire")
-    wire_count = lax.axis_size("wire")
+    wire_here = lax.axis_index(WIRE)
+    wire_count = lax.axis_size(WIRE)
     extended = jnp.concatenate(
         [
             neighbour_group(search, 2),
@@ -52,7 +66,7 @@
         lax.psum_scatter(image_part, "col", scatter_dimension=1, tiled=True),
     )
     total_rows = jnp.float32(rows * wire_count)
-    gram_total = lax.psum(partial_gram, "wire") / total_rows
+    gram_total = sum_over_wire(partial_gram) / total_rows
     gram_stiff = gram_total[:, :width]
     gram_mass = gram_total[:, width:]
     mine_rows = lax.dynamic_slice_in_dim(ritz, col_here * width, width, 0)
@@ -69,11 +83,12 @@
 
 
 def solution(mesh):
-    placed = (P("wire", "col"), P("wire", None), P("wire", None), P())
+    mesh = Mesh(mesh.devices.reshape(8, 4, 2, 4), WIRE + ("col",))
+    placed = (P(WIRE, "col"), P(WIRE, None), P(WIRE, None), P())
     return jax.shard_map(
         shards,
         mesh=mesh,
         in_specs=placed,
-        out_specs=(P("wire", "col"), P("wire", "col"), P("col"), P(None, "col"), P(None, "col")),
+        out_specs=(P(WIRE, "col"), P(WIRE, "col"), P("col"), P(None, "col"), P(None, "col")),
         check_vma=False,
     )

time: 371 us -> 237 us (0.64)
  waiting for transfers between devices: 285 us -> 101 us
  blocking collectives: 0 us -> 34.5 us
  local copies, waits for them, and re-layouts: 30.9 us -> 38.8 us
  starting transfers between devices: 9.98 us -> 15.7 us
    psum x1 -> x0, waiting for transfers between devices: 182 us -> none  [shards(): gram_total = lax.psum(partial_gram, 'wire') / total_rows]
    all_to_all x0 -> x2, blocking collectives: none -> 34.5 us  [the longest x1 18.5 us: sum_over_wire(): part = jnp.sum(lax.all_to_all(flat, RING, 0, 0, tiled=True), axis=0)]
    unnamed x6 -> x5, waiting for transfers between devices: 12.9 us -> 3.96 us
    all_to_all x0 -> x1, waiting for transfers between devices: none -> 6.8 us  [sum_over_wire(): return lax.all_to_all(spread, RING, 0, 0, tiled=True).reshape(shape)]
    all_to_all x0 -> x1, starting transfers between devices: none -> 5.62 us  [sum_over_wire(): return lax.all_to_all(spread, RING, 0, 0, tiled=True).reshape(shape)]
    unnamed x19 -> x15, local copies, waits for them, and re-layouts: 9.5 us -> 12.7 us
  transfers between devices with their start and end apart: 9 -> 9, of which waited for: 6 -> 6; matrix products, arithmetic and copies ran while one was open for 13% -> 22% of each run, Pallas kernels for 0% -> 0%
where the time goes in v1:
time: 237 us; the launch traced here: 236 us
  waiting for transfers between devices  101 us (43%)
  local copies, waits for them, and re-layouts  38.8 us (16%)
  blocking collectives  34.5 us (15%)
  matrix products  26.6 us (11%)
  starting transfers between devices  15.7 us (7%)
  between operations  13.8 us (6%)
  other arithmetic  6.25 us (3%)
    reduce_scatter x1, waiting for transfers between devices, shards(): lax.psum_scatter(modes_part, 'col', scatter_dimension=1, tiled=True)  31.6 us
    reduce_scatter x1, waiting for transfers between devices, shards(): lax.psum_scatter(image_part, 'col', scatter_dimension=1, tiled=True)  30.4 us
    ppermute x4, waiting for transfers between devices, shifted(): lax.ppermute(array, axis, [(i, (i + by) % length) for i in range(length)])  27.8 us
    all_to_all x1, blocking collectives, sum_over_wire(): part = jnp.sum(lax.all_to_all(flat, RING, 0, 0, tiled=True), axis=0)  18.5 us
    all_to_all x1, blocking collectives, sum_over_wire(): part = jnp.sum(lax.all_to_all(spread, 'z', 0, 0, tiled=True), axis=0)  16 us
    unnamed x15, local copies, waits for them, and re-layouts  12.7 us
    concatenate x2, local copies, waits for them, and re-layouts, shards(): jnp.concatenate([neighbour_group(search, 2), neighbour_group(search, 1),...  10.5 us
    ppermute x4, starting transfers between devices, shifted(): lax.ppermute(array, axis, [(i, (i + by) % length) for i in range(length)])  9.78 us
  transfers between devices with their start and end apart: 9, of which 6 were waited for; matrix products, arithmetic and copies ran while one was open for 22% of the time, Pallas kernels for 0%

profile of v1, /device:TPU:1, one launch (start us, length us, event | category | flops | bytes accessed | tf_op | source)
XLA Modules:
  0.0 236.3 jit_solution(6048610642772679567)
XLA Ops:
  7.9 2.2 collective-permute-start
  10.1 2.1 collective-permute-start.1
  12.2 5.5 %collective-permute-start.3 = (f32[3072,96]{0,1:T(8,128)}, f32[3072,96]{0,1:T(8,128)}, u32[]{:S(2)}, u32[]{:S(2)}) collective-permute-start(f32[3072,96]{0,1:T(8,128)} %param.4), channel_id=1, source_target_pairs={{0,248},{4,252},{8,0},{12,4},{16,8},{20,12},{24,16},{28,20},{32,24... | collective-permute-start | bytes 3538952 | tf_op jit(solution)/shard_map/ppermute | solution.py:9
  18.6 24.2 %collective-permute-done = f32[3072,96]{0,1:T(8,128)} collective-permute-done((f32[3072,96]{0,1:T(8,128)}, f32[3072,96]{0,1:T(8,128)}, u32[]{:S(2)}, u32[]{:S(2)}) %collective-permute-start) | collective-permute-done | bytes 1179680 | tf_op jit(solution)/shard_map/ppermute | solution.py:9
  42.8 2.4 %constant_dynamic-update-slice_fusion.4 = f32[15360,96]{0,1:T(8,128)} fusion(f32[3072,96]{0,1:T(8,128)} %collective-permute-done), kind=kLoop, calls=%fused_computation.21 | loop fusion | bytes 2359296
  45.2 3.6 %collective-permute-done.1 = f32[3072,96]{0,1:T(8,128)} collective-permute-done((f32[3072,96]{0,1:T(8,128)}, f32[3072,96]{0,1:T(8,128)}, u32[]{:S(2)}, u32[]{:S(2)}) %collective-permute-start.1) | collective-permute-done | bytes 1179680 | tf_op jit(solution)/shard_map/ppermute | solution.py:9
  48.9 2.4 %constant_dynamic-update-slice_fusion.3 = f32[15360,96]{0,1:T(8,128)} fusion(f32[15360,96]{0,1:T(8,128)} %constant_dynamic-update-slice_fusion.4, f32[3072,96]{0,1:T(8,128)} %collective-permute-done.1), kind=kLoop, calls=%fused_computation.20 | loop fusion | bytes 2359296
  51.3 1.1 constant_dynamic-update-slice_fusion.2
  52.4 2.4 %constant_dynamic-update-slice_fusion.1 = f32[15360,96]{0,1:T(8,128)} fusion(f32[15360,96]{0,1:T(8,128)} %constant_dynamic-update-slice_fusion.2, f32[3072,96]{0,1:T(8,128)} %collective-permute-done.2), kind=kLoop, calls=%fused_computation.18 | loop fusion | bytes 2359296
  54.8 2.4 %constant_dynamic-update-slice_fusion = f32[15360,96]{0,1:T(8,128)} fusion(f32[15360,96]{0,1:T(8,128)} %constant_dynamic-update-slice_fusion.1, f32[3072,96]{0,1:T(8,128)} %collective-permute-done.3), kind=kLoop, calls=%fused_computation.17 | loop fusion | bytes 2359296 | tf_op jit(solution)/shard_map/concatenate | solution.py:39
  57.2 8.2 %copy.24 = f32[15360,96]{1,0:T(8,128)} copy(f32[15360,96]{0,1:T(8,128)} %constant_dynamic-update-slice_fusion) | data formatting | bytes 11796480 | tf_op jit(solution)/shard_map/concatenate | solution.py:39
  65.3 6.9 %gather_fusion = f32[192,64,96]{2,1,0:T(8,128)} fusion(f32[240,64,96]{2,1,0:T(8,128)} %bitcast.24, s32[1024]{0:T(1024)S(1)} %pad_clamp_fusion), kind=kCustom, calls=%fused_computation | custom fusion | bytes 9437952 | tf_op jit(solution)/shard_map/gather | solution.py:53
  72.2 7.2 %fusion.23 = f32[48,96,64]{1,2,0:T(8,128)} fusion(f32[48,256,96]{2,1,0:T(8,128)} %bitcast.25, f32[48,64,256]{2,1,0:T(8,128)S(1)} %bitcast.23), kind=kOutput, calls=%fused_computation.43 | convolution fusion | flops 905969664 | bytes 9043968 | tf_op jit(solution)/shard_map/bik,bkc->bic/dot_general | solution.py:55
  79.5 2.9 %copy.27 = f32[3072,96]{0,1:T(8,128)} copy(f32[3072,96]{1,0:T(8,128)} %bitcast.26) | data formatting | bytes 2359296 | tf_op jit(solution)/shard_map/reshape | solution.py:55
  82.4 2.8 %multiply_add_fusion = f32[3072,96]{0,1:T(8,128)} fusion(f32[3072,96]{0,1:T(8,128)} %copy.27, f32[3072,96]{0,1:T(8,128)} %param.4), kind=kLoop, calls=%fused_computation.6 | loop fusion | flops 589824 | bytes 3538944 | tf_op jit(solution)/shard_map/add | solution.py:56
  85.2 8.6 %fusion.4 = f32[384,192]{0,1:T(8,128)} fusion(f32[3072,384]{0,1:T(8,128)} %all-gather.2.cloned.1.call-done, f32[3072,96]{0,1:T(8,128)} %param.4, f32[3072,96]{0,1:T(8,128)} %multiply_add_fusion), kind=kOutput, calls=%fused_computation.7 | convolution fusion | flops 2718498816 | bytes 7372800 | tf_op jit(solution)/shard_map/rk,rc->kc/dot_general | solution.py:58
  93.8 1.1 copy.28
  95.9 18.5 %all_to_all.15 = f32[8,72,128]{2,1,0:T(8,128)S(1)} all-to-all(f32[8,72,128]{2,1,0:T(8,128)} %reshape.35), channel_id=1, replica_groups=mesh['z'=8,'y'=4,'core'=2,'col'=4] {'y','core'}, dimensions={0} | all-to-all | bytes 589824 | tf_op jit(solution)/shard_map/all_to_all | solution.py:19
  114.4 16.0 %all_to_all.16 = f32[8,72,128]{2,1,0:T(8,128)S(1)} all-to-all(f32[8,72,128]{2,1,0:T(8,128)S(1)} %broadcast_in_dim.7), channel_id=1, replica_groups=mesh['z'=8,'y'=4,'core'=2,'col'=4] {'z'}, dimensions={0} | all-to-all | bytes 589824 | tf_op jit(solution)/shard_map/all_to_all | solution.py:21
  131.1 5.6 %all-to-all-start.2 = ((f32[8,72,128]{2,1,0:T(8,128)}), f32[8,72,128]{2,1,0:T(8,128)S(1)}, u32[]{:S(2)}, u32[]{:S(2)}) async-start(f32[8,72,128]{2,1,0:T(8,128)} %broadcast_in_dim.8), calls=%async_computation.4 | async-start | bytes 589824 | tf_op jit(solution)/shard_map/all_to_all | solution.py:23
  136.8 6.8 %all-to-all-done.2 = f32[8,72,128]{2,1,0:T(8,128)S(1)} async-done(((f32[8,72,128]{2,1,0:T(8,128)}), f32[8,72,128]{2,1,0:T(8,128)S(1)}, u32[]{:S(2)}, u32[]{:S(2)}) %all-to-all-start.2) | async-done | bytes 294944 | tf_op jit(solution)/shard_map/all_to_all | solution.py:23
  144.3 1.1 div.22
  145.4 1.4 fusion.7
  146.8 1.5 fusion.8
  149.4 3.9 %convolution_bitcast_fusion = f32[3072,128]{0,1:T(8,128)} fusion(f32[3072,96]{0,1:T(8,128)} %param.4, f32[384,128]{1,0:T(8,128)} %param.7, s32[]{:T(128)S(6)} %select_n.23), kind=kOutput, calls=%fused_computation.1 | convolution fusion | flops 452984832 | bytes 2801668 | tf_op jit(solution)/shard_map/dot_general | solution.py:62
  153.4 3.9 %fusion.9 = f32[3072,128]{0,1:T(8,128)} fusion(f32[3072,96]{0,1:T(8,128)} %multiply_add_fusion, f32[384,128]{1,0:T(8,128)} %param.7, s32[]{:T(128)S(6)} %select_n.23), kind=kOutput, calls=%fused_computation.14 | convolution fusion | flops 452984832 | bytes 2801668 | tf_op jit(solution)/shard_map/dot_general | solution.py:63
  158.1 1.7 copy.29
  159.8 1.7 copy.30
  161.5 3.2 %reduce-scatter.10.cloned.1.call-done = f32[32,2]{1,0:T(8,128)} async-done(((f32[128,2]{1,0:T(8,128)}), f32[32,2]{1,0:T(8,128)}) %reduce-scatter.10.cloned.1.call-update) | async-done | bytes 272
  165.8 31.6 %reduce-scatter.6.cloned.1.call-done = f32[3072,32]{0,1:T(8,128)} async-done(((f32[3072,128]{0,1:T(8,128)}), f32[3072,32]{0,1:T(8,128)}) %reduce-scatter.6.cloned.1.call-update) | async-done | bytes 393232 | tf_op jit(solution)/shard_map/reduce_scatter | solution.py:65
  197.3 30.4 %reduce-scatter.8.cloned.1.call-done = f32[3072,32]{0,1:T(8,128)} async-done(((f32[3072,128]{0,1:T(8,128)}), f32[3072,32]{0,1:T(8,128)}) %reduce-scatter.8.cloned.1.call-update) | async-done | bytes 393232 | tf_op jit(solution)/shard_map/reduce_scatter | solution.py:66
  227.8 2.0 multiply_subtract_fusion
  (35 shorter events, 7.0 us)
Async XLA Ops:
  7.2 65.1 %copy-start = (f32[3072,256]{1,0:T(8,128)S(1)}, f32[3072,256]{1,0:T(8,128)}, u32[]{:S(2)}) copy-start(f32[3072,256]{1,0:T(8,128)} %param.5) | copy-start | bytes 9437188
  7.2 78.0 %all-gather.2.cloned.1.call-start = ((), (), s32[]{:S(2)}) async-start(), calls=%async_computation.8 | async-start | bytes 5898240 | tf_op jit(solution)/shard_map/all_gather | solution.py:59
  7.9 34.9 %collective-permute-start = (f32[3072,96]{0,1:T(8,128)}, f32[3072,96]{0,1:T(8,128)}, u32[]{:S(2)}, u32[]{:S(2)}) collective-permute-start(f32[3072,96]{0,1:T(8,128)} %param.4), channel_id=1, source_target_pairs={{0,8},{4,12},{8,16},{12,20},{16,24},{20,28},{24,32},{28,36},{32,40... | collective-permute-start | bytes 3538952 | tf_op jit(solution)/shard_map/ppermute | solution.py:9
  10.1 38.7 %collective-permute-start.1 = (f32[3072,96]{0,1:T(8,128)}, f32[3072,96]{0,1:T(8,128)}, u32[]{:S(2)}, u32[]{:S(2)}) collective-permute-start(f32[3072,96]{0,1:T(8,128)} %param.4), channel_id=1, source_target_pairs={{0,4},{4,8},{8,12},{12,16},{16,20},{20,24},{24,28},{28,32},{32,36}... | collective-permute-start | bytes 3538952 | tf_op jit(solution)/shard_map/ppermute | solution.py:9
  12.2 40.2 %collective-permute-start.2 = (f32[3072,96]{0,1:T(8,128)}, f32[3072,96]{0,1:T(8,128)}, u32[]{:S(2)}, u32[]{:S(2)}) collective-permute-start(f32[3072,96]{0,1:T(8,128)} %param.4), channel_id=1, source_target_pairs={{0,252},{4,0},{8,4},{12,8},{16,12},{20,16},{24,20},{28,24},{32,28}... | collective-permute-start | bytes 3538952 | tf_op jit(solution)/shard_map/ppermute | solution.py:9
  12.2 42.5 %collective-permute-start.3 = (f32[3072,96]{0,1:T(8,128)}, f32[3072,96]{0,1:T(8,128)}, u32[]{:S(2)}, u32[]{:S(2)}) collective-permute-start(f32[3072,96]{0,1:T(8,128)} %param.4), channel_id=1, source_target_pairs={{0,248},{4,252},{8,0},{12,4},{16,8},{20,12},{24,16},{28,20},{32,24... | collective-permute-start | bytes 3538952 | tf_op jit(solution)/shard_map/ppermute | solution.py:9
  18.6 32.6 %copy-start.1 = (f32[3072,96]{0,1:T(8,128)S(1)}, f32[3072,96]{0,1:T(8,128)}, u32[]{:S(2)}) copy-start(f32[3072,96]{0,1:T(8,128)} %param.4) | copy-start | bytes 3538948
  131.1 12.4 %all-to-all-start.2 = ((f32[8,72,128]{2,1,0:T(8,128)}), f32[8,72,128]{2,1,0:T(8,128)S(1)}, u32[]{:S(2)}, u32[]{:S(2)}) async-start(f32[8,72,128]{2,1,0:T(8,128)} %broadcast_in_dim.8), calls=%async_computation.4 | async-start | bytes 589824 | tf_op jit(solution)/shard_map/all_to_all | solution.py:23
  136.7 28.0 %reduce-scatter.10.cloned.1.call-start = ((), (), s32[]{:S(2)}) async-start(), calls=%async_computation.9 | async-start | bytes 81920
  149.1 48.2 %reduce-scatter.6.cloned.1.call-start = ((), (), s32[]{:S(2)}) async-start(), calls=%async_computation.6 | async-start | bytes 1966080 | tf_op jit(solution)/shard_map/reduce_scatter | solution.py:65
  153.3 74.5 %reduce-scatter.8.cloned.1.call-start = ((), (), s32[]{:S(2)}) async-start(), calls=%async_computation.7 | async-start | bytes 1966080 | tf_op jit(solution)/shard_map/reduce_scatter | solution.py:66
  165.8 64.0 %copy-start.2 = (f32[32]{0:T(128)}, f32[32]{0:T(128)S(1)}, u32[]{:S(2)}) copy-start(f32[32]{0:T(128)S(1)} %divide_bitcast_fusion) | copy-start | bytes 388
Sparse Core Ops, SparseCore 0:
  9.8 58.6 all-gather.1
  149.2 15.4 reduce-scatter.9
  167.9 29.4 reduce-scatter.5
  199.8 27.9 reduce-scatter.7
